TPU v7x, 128 devices: a whole 4x4x4 slice. The times are simulated.
128 devices in a mesh: dp: 8 (over z_lo, x), tensor: 16 (over z_hi, y, core).
Axes of the slice: x: 4, y: 4, z: 4 (z_hi: 2, z_lo: 2; z = z_hi * 2 + z_lo), core: 2. Of those that a mesh axis runs over, the one named last changes fastest.
Arguments:
- saved_inputs: bfloat16 [3072, 6144], P(('dp', 'tensor')), may hold values from -24 to 24
- hidden_grads: bfloat16 [3072, 24576], P('dp', 'tensor'), may hold values from -6 to 6
- up_weight: bfloat16 [6144, 24576], P(None, 'tensor'), may hold values from -0.078125 to 0.078125
- up_bias: float32 [24576], P('tensor'), may hold values from -1 to 1
Outputs:
- input_grads: bfloat16 [3072, 6144], P(('dp', 'tensor'))
- weight_grads: bfloat16 [6144, 24576], P('dp', 'tensor')
All inputs are finite; a program needn't handle non-finite values.
Results may differ from a plain program's by a relative error of at most 0.014.
Values may be sent and summed in bfloat16 or wider, within the bound.
A program may use at most 128 MiB of HBM per device.

v0:
```python
import jax
import jax.numpy as jnp
from jax import lax
from jax.sharding import PartitionSpec as P


def from_everyone(x, axis):
    length = lax.axis_size(axis)
    return lax.all_to_all(jnp.broadcast_to(x[None], (length, *x.shape)), axis, 0, 0, tiled=True)


def in_order(pieces, dim):
    pieces = jnp.moveaxis(pieces, 0, dim)
    shape = pieces.shape
    return pieces.reshape(*shape[:dim], shape[dim] * shape[dim + 1], *shape[dim + 2 :])


def gathered_copies(x, axis, dim):
    pieces = from_everyone(x, axis)
    return in_order(pieces, dim)


def slope(pre):
    cdf = 0.5 * (1.0 + jax.scipy.special.erf(pre * 0.7071067811865476))
    pdf = jnp.exp(-0.5 * pre * pre) * 0.3989422804014327
    return cdf + pre * pdf


def body(saved_inputs, hidden_grads, up_weight, up_bias):
    gathered = lax.all_gather(saved_inputs, "tensor", axis=0, tiled=True)
    pre = jnp.dot(gathered, up_weight, preferred_element_type=jnp.float32) + up_bias
    local_grads = (hidden_grads.astype(jnp.float32) * slope(pre)).astype(jnp.bfloat16)
    input_grads = lax.psum_scatter(
        lax.dot_general(
            local_grads, up_weight, (((1,), (1,)), ((), ())), preferred_element_type=jnp.float32
        ).astype(jnp.bfloat16),
        "tensor",
        scatter_dimension=0,
        tiled=True,
    )
    replica_rows = gathered.shape[0]
    replicas = lax.axis_size("dp")
    factor = 1.0 / jnp.sqrt(jnp.float32(replica_rows * replicas))
    own_rows = up_weight.shape[0] // replicas
    blocks = lax.all_to_all(gathered, "dp", split_axis=1, concat_axis=0, tiled=True)
    piece = gathered_copies(local_grads, "dp", 0)
    groups = piece.shape[0] // replica_rows
    parts = jnp.einsum(
        "rtd,rtf->rdf",
        blocks.reshape(groups, replica_rows, own_rows),
        piece.reshape(groups, replica_rows, piece.shape[1]),
        preferred_element_type=jnp.float32,
    )
    rounded = lax.optimization_barrier(parts.astype(jnp.bfloat16))
    summed = jnp.sum(rounded.astype(jnp.float32), axis=0)
    weight_grads = (summed * factor).astype(jnp.bfloat16)
    return (input_grads, weight_grads)


def solution(mesh):
    return jax.shard_map(
        body,
        mesh=mesh,
        in_specs=(P(("dp", "tensor"), None), P("dp", "tensor"), P(None, "tensor"), P("tensor")),
        out_specs=(P(("dp", "tensor"), None), P("dp", "tensor")),
        check_vma=False,
    )
```

profile of v0, /device:TPU:6, one launch (start us, length us, event | category | flops | bytes accessed | tf_op | source)
XLA Modules:
  0.0 346.3 jit_solution(11939431683800678526)
XLA Ops:
  7.2 0.0 all-gather.2.cloned.1.call-start
  7.2 0.7 all-gather.2.cloned.1.call-update
  7.9 63.0 %all-gather.2.cloned.1.call-done = bf16[384,6144]{1,0:T(8,128)(2,1)} async-done(((bf16[24,6144]{1,0:T(8,128)(2,1)}), bf16[384,6144]{1,0:T(8,128)(2,1)}) %all-gather.2.cloned.1.call-update) | async-done | bytes 4718608 | tf_op jit(solution)/shard_map/all_gather | solution.py:30
  70.9 6.6 %copy.11 = bf16[384,6144]{0,1:T(8,128)(2,1)} copy(bf16[384,6144]{1,0:T(8,128)(2,1)} %all-gather.2.cloned.1.call-done) | data formatting | bytes 9437184 | tf_op jit(solution)/shard_map/all_gather | solution.py:30
  77.5 6.7 %copy.12 = bf16[384,8,768]{2,0,1:T(8,128)(2,1)} copy(bf16[384,8,768]{0,2,1:T(8,128)(2,1)} %bitcast.11) | data formatting | bytes 9437184 | tf_op jit(solution)/shard_map/all_to_all | solution.py:45
  84.2 0.0 copy-start
  84.2 0.0 copy-start.1
  84.2 5.2 %all-to-all-start.1 = ((bf16[384,8,768]{2,0,1:T(8,128)(2,1)}), bf16[384,8,768]{2,0,1:T(8,128)(2,1)}, u32[]{:S(2)}, u32[]{:S(2)}) async-start(bf16[384,8,768]{2,0,1:T(8,128)(2,1)} %copy.12), calls=%async_computation.2 | async-start | bytes 9437184 | tf_op jit(solution)/shard_map/all_to_all | solution.py:45
  89.4 0.0 copy-done
  89.4 0.0 copy-done.1
  89.4 13.4 %fusion.6 = bf16[384,1536]{1,0:T(8,128)(2,1)S(1)} fusion(bf16[384,6144]{1,0:T(8,128)(2,1)} %all-gather.2.cloned.1.call-done, bf16[6144,1536]{1,0:T(8,128)(2,1)} %param.6, bf16[384,1536]{1,0:T(8,128)(2,1)S(1)} %copy-done, f32[1536]{0:T(1024)S(1)} %copy-done.1), kind=kOutput, calls=%fused_computation.12 | convolution fusion | flops 7254835200 | bytes 25958400 | tf_op jit(solution)/shard_map/dot_general | solution.py:31
  102.7 0.7 copy.10
  103.5 56.3 %all-to-all-done.1 = bf16[384,8,768]{2,0,1:T(8,128)(2,1)} async-done(((bf16[384,8,768]{2,0,1:T(8,128)(2,1)}), bf16[384,8,768]{2,0,1:T(8,128)(2,1)}, u32[]{:S(2)}, u32[]{:S(2)}) %all-to-all-start.1) | async-done | bytes 4718624 | tf_op jit(solution)/shard_map/all_to_all | solution.py:45
  159.8 4.4 %broadcast_in_dim.2 = bf16[8,384,1536]{1,2,0:T(8,128)(2,1)} broadcast(bf16[384,1536]{0,1:T(8,128)(2,1)S(1)} %copy.10), dimensions={1,2} | broadcast | bytes 10616832 | tf_op jit(solution)/shard_map/broadcast_in_dim | solution.py:9
  164.3 5.4 %all-to-all-start = ((bf16[8,384,1536]{1,2,0:T(8,128)(2,1)}), bf16[8,384,1536]{1,2,0:T(8,128)(2,1)}, u32[]{:S(2)}, u32[]{:S(2)}) async-start(bf16[8,384,1536]{1,2,0:T(8,128)(2,1)} %broadcast_in_dim.2), calls=%async_computation.1 | async-start | bytes 18874368 | tf_op jit(solution)/shard_map/all_to_all | solution.py:9
  169.7 0.0 reduce-scatter.2.cloned.1.call-start
  169.7 12.8 %convolution_convert_fusion = bf16[384,6144]{1,0:T(8,128)(2,1)} fusion(bf16[384,1536]{1,0:T(8,128)(2,1)S(1)} %fusion.6, bf16[6144,1536]{1,0:T(8,128)(2,1)} %param.6), kind=kOutput, calls=%fused_computation.2 | convolution fusion | flops 7250116608 | bytes 24772608 | tf_op jit(solution)/shard_map/dot_general | solution.py:34
  182.5 0.0 reduce-scatter.2.cloned.1.call-update
  182.5 126.0 %all-to-all-done = bf16[8,384,1536]{1,2,0:T(8,128)(2,1)} async-done(((bf16[8,384,1536]{1,2,0:T(8,128)(2,1)}), bf16[8,384,1536]{1,2,0:T(8,128)(2,1)}, u32[]{:S(2)}, u32[]{:S(2)}) %all-to-all-start) | async-done | bytes 9437216 | tf_op jit(solution)/shard_map/all_to_all | solution.py:9
  308.6 17.6 %convert_bitcast_fusion = bf16[8,768,1536]{1,2,0:T(8,128)(2,1)} fusion(bf16[8,384,1536]{1,2,0:T(8,128)(2,1)} %all-to-all-done, bf16[384,8,768]{2,0,1:T(8,128)(2,1)} %all-to-all-done.1), kind=kOutput, calls=%fused_computation.1 | convolution fusion | flops 7257194496 | bytes 33030144 | tf_op jit(solution)/shard_map/rtd,rtf->rdf/dot_general | solution.py:48
  326.1 10.4 %convert_reduce_fusion = f32[768,1536]{0,1:T(8,128)S(1)} fusion(bf16[8,768,1536]{1,2,0:T(8,128)(2,1)} %convert_bitcast_fusion), kind=kLoop, calls=%fused_computation | loop fusion | flops 17694720 | bytes 23592960 | tf_op jit(solution)/shard_map/reduce_sum | solution.py:55
  336.5 0.5 multiply_convert_fusion
  337.0 2.4 copy.13
  339.4 0.0 reduce-scatter.2.cloned.1.call-done
Async XLA Ops:
  7.2 63.8 %all-gather.2.cloned.1.call-start = ((), (), s32[]{:S(2)}) async-start(), calls=%async_computation.3 | async-start | bytes 5013504 | tf_op jit(solution)/shard_map/all_gather | solution.py:30
  84.2 5.2 %copy-start = (bf16[384,1536]{1,0:T(8,128)(2,1)S(1)}, bf16[384,1536]{1,0:T(8,128)(2,1)}, u32[]{:S(2)}) copy-start(bf16[384,1536]{1,0:T(8,128)(2,1)} %param.5) | copy-start | bytes 3538948
  84.2 5.2 %copy-start.1 = (f32[1536]{0:T(1024)S(1)}, f32[1536]{0:T(1024)}, u32[]{:S(2)}) copy-start(f32[1536]{0:T(1024)} %param.7) | copy-start | bytes 18436
  84.2 75.6 %all-to-all-start.1 = ((bf16[384,8,768]{2,0,1:T(8,128)(2,1)}), bf16[384,8,768]{2,0,1:T(8,128)(2,1)}, u32[]{:S(2)}, u32[]{:S(2)}) async-start(bf16[384,8,768]{2,0,1:T(8,128)(2,1)} %copy.12), calls=%async_computation.2 | async-start | bytes 9437184 | tf_op jit(solution)/shard_map/all_to_all | solution.py:45
  164.3 144.3 %all-to-all-start = ((bf16[8,384,1536]{1,2,0:T(8,128)(2,1)}), bf16[8,384,1536]{1,2,0:T(8,128)(2,1)}, u32[]{:S(2)}, u32[]{:S(2)}) async-start(bf16[8,384,1536]{1,2,0:T(8,128)(2,1)} %broadcast_in_dim.2), calls=%async_computation.1 | async-start | bytes 18874368 | tf_op jit(solution)/shard_map/all_to_all | solution.py:9
  169.7 169.7 %reduce-scatter.2.cloned.1.call-start = ((), (), s32[]{:S(2)}) async-start(), calls=%async_computation.4 | async-start | bytes 5013504 | tf_op jit(solution)/shard_map/reduce_scatter | solution.py:33
Sparse Core Ops, SparseCore 0:
  10.4 60.4 all-gather.1
  182.7 134.7 reduce-scatter.1
where the time goes:
time: 347 us; the launch traced here: 346 us
  waiting for transfers between devices  246 us (71%)
  matrix products  43.7 us (13%)
  local copies, waits for them, and re-layouts  20.9 us (6%)
  between operations  14.1 us (4%)
  other arithmetic  10.9 us (3%)
  starting transfers between devices  10.6 us (3%)
    all_to_all x1, waiting for transfers between devices, from_everyone(): lax.all_to_all(jnp.broadcast_to(x[None], (length, *x.shape)), axis, 0, 0,...  126 us
    all_gather x1, waiting for transfers between devices, body(): gathered = lax.all_gather(saved_inputs, 'tensor', axis=0, tiled=True)  63 us
    all_to_all x1, waiting for transfers between devices, body(): lax.all_to_all(gathered, 'dp', split_axis=1, concat_axis=0, tiled=True)  56.3 us
    dot_general x1, matrix products, body(): jnp.einsum('rtd,rtf->rdf', blocks.reshape(groups, replica_rows, own_rows)...  17.6 us
    dot_general x1, matrix products, body(): jnp.dot(gathered, up_weight, preferred_element_type=jnp.float32) + up_bias  13.4 us
    dot_general x1, matrix products, body(): lax.dot_general(local_grads, up_weight, (((1,), (1,)), ((), ())), preferr...  12.8 us
    reduce_sum x1, other arithmetic, body(): summed = jnp.sum(rounded.astype(jnp.float32), axis=0)  10.4 us
  transfers between devices with their start and end apart: 4, of which 3 were waited for; matrix products, arithmetic and copies ran while one was open for 17% of the time, Pallas kernels for 0%

commit v1 on v0

v1 whole, which is shorter than its diff:
```python
import functools

import jax
import jax.numpy as jnp
from jax import lax
from jax.experimental import pallas as pl
from jax.experimental.pallas import tpu as pltpu
from jax.sharding import PartitionSpec as P

MESH = pl.DeviceIdType.MESH
F32 = jnp.float32
BF16 = jnp.bfloat16

PIECES = 2
CHUNKS = 6

SWAP = 0
FIRST = 1
SECOND = FIRST + 17 * PIECES
EXCHANGE = SECOND + 17
GRADS = EXCHANGE + 4
HALVES = GRADS + 9 * CHUNKS
SCATTER = HALVES + CHUNKS
MESSAGES = SCATTER + 8


def slope(pre):
    cdf = 0.5 * (1.0 + lax.erf(pre * 0.7071067811865476))
    pdf = jnp.exp(-0.5 * pre * pre) * 0.3989422804014327
    return cdf + pre * pdf


class Gather:
    def __init__(self, post, await_, number, view, q, p, ring, pair, twin=None, mine=0, other=0):
        self.post, self.await_, self.number, self.view = post, await_, number, view
        self.q, self.p, self.ring, self.pair = q, p, ring, pair
        self.twin, self.mine, self.other = twin, mine, other

    def move(self, m, k, q, p, part, device):
        view = self.view(self.mine, q % 2, p % 4, part, k)
        self.post(self.number(m, k), view, view, device)

    def landed(self, m, k, q, p, part):
        self.await_(self.number(m, k), self.view(self.mine, q % 2, p % 4, part, k))

    def hand(self, m, k, q, p):
        if self.twin is not None:
            self.move(m, k, q, p, 2, self.twin)

    def own(self, k):
        q, p = self.q, self.p
        self.move(0, k, q, p, 2, self.pair)
        self.move(1, k, q, p, 2, self.ring(1))
        self.move(2, k, q, p, 2, self.ring(3))
        self.hand(9, k, q, p)

    def paired(self, k):
        q, p = self.q + 1, self.p
        self.landed(0, k, q, p, 2)
        self.move(3, k, q, p, 2, self.ring(1))
        self.move(4, k, q, p, 2, self.ring(3))
        self.hand(10, k, q, p)

    def halves(self, k, q, m, forward, hand):
        p = self.p
        self.landed(m, k, q, p + 3, 2)
        self.move(forward, k, q, p + 3, 0, self.ring(1))
        self.landed(m + 1, k, q, p + 1, 2)
        self.move(forward + 1, k, q, p + 1, 1, self.ring(3))
        self.hand(hand, k, q, p + 3)
        self.hand(hand + 1, k, q, p + 1)

    def near(self, k):
        self.halves(k, self.q, 1, 5, 11)

    def near_paired(self, k):
        self.halves(k, self.q + 1, 3, 7, 13)

    def far(self, k):
        self.landed(5, k, self.q, self.p + 2, 0)
        self.landed(6, k, self.q, self.p + 2, 1)
        self.hand(15, k, self.q, self.p + 2)

    def far_paired(self, k):
        self.landed(7, k, self.q + 1, self.p + 2, 0)
        self.landed(8, k, self.q + 1, self.p + 2, 1)
        self.hand(16, k, self.q + 1, self.p + 2)

    def handed(self, k):
        q, p = self.q, self.p
        places = ((q, p), (q + 1, p), (q, p + 3), (q, p + 1), (q + 1, p + 3), (q + 1, p + 1), (q, p + 2), (q + 1, p + 2))
        for i, (a, b) in enumerate(places):
            self.await_(self.number(9 + i, k), self.view(self.other, a % 2, b % 4, 2, k))

    def drain(self, drained, k):
        q, p = self.q, self.p
        parts = [2] * 5 + [0, 1, 0, 1] + ([2] * 8 if self.twin is not None else [])
        for m, part in enumerate(parts):
            drained(self.number(m, k), self.view(self.mine, q, p, part, k))


def kernel(
    factor, x_ref, hidden_hbm, weight_hbm, bias_ref, inputs_out, weights_out,
    weight, hidden, xr, xb, grads, partial, twin_part, near_part, next_part, pair_part, total, swap, share, final,
    sends, receives, loads,
):
    d, t = lax.axis_index("dp"), lax.axis_index("tensor")
    zl, x, zh, y, c = d // 4, d % 4, t // 8, (t // 2) % 4, t % 2
    o = 1 - c
    rows, model = x_ref.shape
    half = model // 2
    tokens, units = hidden.shape
    width = units // CHUNKS
    piece = half // PIECES
    block = model // 8
    step = half // CHUNKS

    def at(zl_, x_, zh_, y_, c_):
        return (zl_ * 4 + x_ % 4, zh_ * 8 + (y_ % 4) * 2 + c_)

    twin = at(zl, x, zh, y, o)
    pair_h = at(zl, x, 1 - zh, y, c)
    pair_l = at(1 - zl, x, zh, y, c)

    def ring_y(k):
        return at(zl, x, zh, y + k, c)

    def ring_x(k):
        return at(zl, x + k, zh, y, c)

    def post(m, src, dst, device):
        pltpu.make_async_remote_copy(
            src_ref=src, dst_ref=dst, send_sem=sends.at[m], recv_sem=receives.at[m], device_id=device, device_id_type=MESH
        ).start()

    def described(m, ref):
        return pltpu.make_async_remote_copy(
            src_ref=ref, dst_ref=ref, send_sem=sends.at[m], recv_sem=receives.at[m], device_id=twin, device_id_type=MESH
        )

    def landed(m, ref):
        described(m, ref).wait_recv()

    def drained(m, ref):
        described(m, ref).wait_send()

    def weight_load(j, h):
        part = pl.ds(h * half + j * piece, piece)
        return pltpu.make_async_copy(weight_hbm.at[part], weight.at[part], loads.at[2 * j + h])

    for j in range(PIECES):
        for h in range(2):
            weight_load(j, h).start()
    hidden_load = pltpu.make_async_copy(hidden_hbm, hidden, loads.at[2 * PIECES])
    hidden_load.start()

    barrier = pltpu.get_barrier_semaphore()
    greeted = [twin, pair_h, pair_l, ring_y(1), ring_y(3), ring_x(1), ring_x(3)]
    greeted += [at(o, x + k, zh, y, zl) for k in range(4)]
    for device in greeted:
        pl.semaphore_signal(barrier, inc=1, device_id=device, device_id_type=MESH)
    pl.semaphore_wait(barrier, len(greeted))

    own_half = pl.ds(pl.multiple_of(c * half, half), half)
    other_half = pl.ds(pl.multiple_of(o * half, half), half)
    post(SWAP, x_ref.at[:, other_half], swap, twin)
    mine = x_ref[:, own_half].astype(F32)
    landed(SWAP, swap)
    theirs = swap[...].astype(F32)
    upper = jnp.where(c == 0, mine, theirs)
    lower = jnp.where(c == 0, theirs, mine)
    xr[c, zh, y] = jnp.concatenate([upper, lower], axis=0).astype(BF16)

    def view_first(h, q, p, part, j):
        cols = (pl.ds(j * piece, piece // 2), pl.ds(j * piece + piece // 2, piece // 2), pl.ds(j * piece, piece))[part]
        return xr.at[h, q, p, :, cols]

    def view_second(h, q, p, part, j):
        return xb.at[h, q, p, (pl.ds(0, 2), pl.ds(2, 2), pl.ds(0, 4))[part]]

    def view_grads(h, q, p, part, k):
        near, all_ = tokens // 2, tokens
        lines = (pl.ds(0, near), pl.ds(near, near), pl.ds(0, all_))[part]
        return grads.at[q, p, lines, pl.ds(pl.multiple_of(k * width, width), width)]

    first = Gather(post, landed, lambda m, j: FIRST + 17 * j + m, view_first, zh, y, ring_y, pair_h, twin, c, o)
    second = Gather(post, landed, lambda m, j: SECOND + m, view_second, zh, y, ring_y, pair_h, twin, o, c)
    third = Gather(post, landed, lambda m, k: GRADS + CHUNKS * m + k, view_grads, zl, x, ring_x, pair_l)

    for j in range(PIECES):
        first.own(j)
    for k in range(4):
        cols = pl.ds(pl.multiple_of(((x + k) % 4) * block, block), block)
        post(EXCHANGE + k, xr.at[c, zh, y, :, cols], xb.at[zl, zh, y, x], at(c, x + k, zh, y, 1 - zl))

    for j in range(PIECES):
        first.paired(j)
    for j in range(PIECES):
        first.near(j)
    for k in range(4):
        landed(EXCHANGE + k, xb.at[o, zh, y, (x + 4 - k) % 4])

    def forward(j, n):
        cols = pl.ds(pl.multiple_of(n * width, width), width)
        out = None
        for h in range(2):
            a = xr[h, :, :, :, j * piece : (j + 1) * piece].reshape(tokens, piece)
            term = jnp.dot(a, weight[h * half + j * piece : h * half + (j + 1) * piece, cols], preferred_element_type=F32)
            out = term if out is None else out + term
        return out

    for j in range(PIECES):
        first.near_paired(j)
        first.far(j)
        first.far_paired(j)
        if j == PIECES - 1:
            second.own(0)
        first.handed(j)
        for h in range(2):
            weight_load(j, h).wait()
        if j < PIECES - 1:

            @pl.loop(0, CHUNKS)
            def _(n):
                cols = pl.ds(pl.multiple_of(n * width, width), width)
                if j == 0:
                    total[0:tokens, cols] = forward(j, n)
                else:
                    total[0:tokens, cols] += forward(j, n)

    hidden_load.wait()

    @pl.loop(0, CHUNKS)
    def _(n):
        cols = pl.ds(pl.multiple_of(n * width, width), width)
        pre = total[0:tokens, cols] + forward(PIECES - 1, n) + bias_ref[:, cols]
        total[0:tokens, cols] = pre
        strip = 32

        @pl.loop(0, tokens // strip)
        def _(s):
            lines = pl.ds(pl.multiple_of(s * strip, strip), strip)
            g = hidden[lines, cols].astype(F32) * slope(total[lines, cols])
            grads[zl, x, lines, cols] = g.astype(BF16)

        third.own(n)

    second.paired(0)
    second.near(0)

    def backward(h, n, w):
        lines = pl.ds(pl.multiple_of(h * half + n * w, w), w)
        return lax.dot_general(grads[zl, x], weight[lines, :], (((1,), (1,)), ((), ())), preferred_element_type=F32)

    narrow = step // 2

    def piece_of(n):
        return pl.ds(pl.multiple_of(n * narrow, narrow), narrow)

    def chunk_of(k):
        return pl.ds(pl.multiple_of(k * step, step), step)

    @pl.loop(0, CHUNKS)
    def _(k):
        third.paired(k)
        third.near(k)

        @pl.loop(0, 2)
        def _(i):
            n = 2 * k + i
            partial[o, :, :, :, piece_of(n)] = backward(o, n, narrow).astype(BF16).reshape(2, 4, 2 * rows, narrow)

        post(HALVES + k, partial.at[o, :, :, :, chunk_of(k)], twin_part.at[:, :, :, chunk_of(k)], twin)

    second.near_paired(0)
    second.far(0)

    @pl.loop(0, CHUNKS)
    def _(k):
        landed(HALVES + k, twin_part.at[:, :, :, chunk_of(k)])

        @pl.loop(0, 2)
        def _(i):
            n = 2 * k + i
            theirs = twin_part[:, :, :, piece_of(n)].reshape(tokens, narrow).astype(F32)
            partial[c, :, :, :, piece_of(n)] = (backward(c, n, narrow) + theirs).astype(BF16).reshape(2, 4, 2 * rows, narrow)

    left, right = pl.ds(0, half // 2), pl.ds(half // 2, half // 2)
    plus, minus, across = (y + 1) % 4, (y + 3) % 4, (y + 2) % 4

    post(SCATTER + 0, partial.at[c, :, across, :, left], near_part.at[0], ring_y(1))
    post(SCATTER + 1, partial.at[c, :, across, :, right], near_part.at[1], ring_y(3))
    post(SCATTER + 2, partial.at[c, :, plus, :, right], next_part.at[0, :, :, right], ring_y(1))
    post(SCATTER + 3, partial.at[c, :, minus, :, left], next_part.at[1, :, :, left], ring_y(3))
    second.far_paired(0)
    second.handed(0)

    def weight_term(q, p, cols):
        a = xb[q % 2, :, :, p % 4].reshape(tokens, block)
        g = grads[q % 2, p % 4, :, cols]
        return lax.dot_general(a, g, (((0,), (0,)), ((), ())), preferred_element_type=F32)

    def add_replica(q, p, start=False):
        @pl.loop(0, CHUNKS)
        def _(n):
            cols = pl.ds(pl.multiple_of(n * width, width), width)
            term = weight_term(q, p, cols)
            if start:
                total[:, cols] = term
            else:
                total[:, cols] += term

    add_replica(zl, x, True)
    third.near_paired(0)

    landed(SCATTER + 0, near_part.at[0])
    partial[c, :, plus, :, left] = (partial[c, :, plus, :, left].astype(F32) + near_part[0].astype(F32)).astype(BF16)
    post(SCATTER + 4, partial.at[c, :, plus, :, left], next_part.at[0, :, :, left], ring_y(1))
    landed(SCATTER + 1, near_part.at[1])
    partial[c, :, minus, :, right] = (partial[c, :, minus, :, right].astype(F32) + near_part[1].astype(F32)).astype(BF16)
    post(SCATTER + 5, partial.at[c, :, minus, :, right], next_part.at[1, :, :, right], ring_y(3))

    add_replica(zl + 1, x)
    third.near_paired(1)
    add_replica(zl, x + 3)
    third.near_paired(2)
    add_replica(zl, x + 1)

    landed(SCATTER + 2, next_part.at[0, :, :, right])
    landed(SCATTER + 3, next_part.at[1, :, :, left])
    landed(SCATTER + 4, next_part.at[0, :, :, left])
    landed(SCATTER + 5, next_part.at[1, :, :, right])

    def reduced(z):
        return partial[c, z, y].astype(F32) + next_part[0, z].astype(F32) + next_part[1, z].astype(F32)

    partial[c, 1 - zh, y] = reduced(1 - zh).astype(BF16)
    post(SCATTER + 6, partial.at[c, 1 - zh, y], pair_part, pair_h)

    @pl.loop(3, CHUNKS)
    def _(k):
        third.near_paired(k)

    landed(SCATTER + 6, pair_part)
    summed = reduced(zh) + pair_part[...].astype(F32)
    upper, lower = summed[0:rows], summed[rows : 2 * rows]
    share[...] = jnp.where(c == 0, lower, upper).astype(BF16)
    post(SCATTER + 7, share, final, twin)
    inputs_out[:, own_half] = jnp.where(c == 0, upper, lower).astype(BF16)

    add_replica(zl + 1, x + 3)
    add_replica(zl + 1, x + 1)
    landed(SCATTER + 7, final)
    inputs_out[:, other_half] = final[...]

    @pl.loop(0, CHUNKS)
    def _(k):
        third.far(k)

    add_replica(zl, x + 2)

    @pl.loop(0, CHUNKS)
    def _(k):
        third.far_paired(k)
        cols = pl.ds(pl.multiple_of(k * width, width), width)
        weights_out[:, cols] = ((total[:, cols] + weight_term(zl + 1, x + 2, cols)) * factor).astype(BF16)

    drained(SWAP, swap)
    for j in range(PIECES):
        first.drain(drained, j)
    second.drain(drained, 0)
    for k in range(4):
        drained(EXCHANGE + k, xb.at[zl, zh, y, x])

    @pl.loop(0, CHUNKS)
    def _(k):
        third.drain(drained, k)
        drained(HALVES + k, twin_part.at[:, :, :, chunk_of(k)])

    for m, ref in enumerate(
        [
            near_part.at[0], near_part.at[1], next_part.at[0, :, :, right], next_part.at[1, :, :, left],
            next_part.at[0, :, :, left], next_part.at[1, :, :, right], pair_part, share,
        ]
    ):
        drained(SCATTER + m, ref)


def body(saved_inputs, hidden_grads, up_weight, up_bias):
    rows, model = saved_inputs.shape
    tokens, units = hidden_grads.shape
    half, block = model // 2, model // 8
    factor = float(1.0 / (tokens * 8) ** 0.5)
    any_space, vmem = pl.BlockSpec(memory_space=pl.ANY), pl.BlockSpec(memory_space=pltpu.VMEM)
    return pl.pallas_call(
        functools.partial(kernel, factor),
        out_shape=(jax.ShapeDtypeStruct((rows, model), BF16), jax.ShapeDtypeStruct((block, units), BF16)),
        in_specs=[vmem, any_space, any_space, vmem],
        out_specs=(vmem, vmem),
        scratch_shapes=[
            pltpu.VMEM((model, units), BF16),
            pltpu.VMEM((tokens, units), BF16),
            pltpu.VMEM((2, 2, 4, 2 * rows, half), BF16),
            pltpu.VMEM((2, 2, 4, 4, 2 * rows, block), BF16),
            pltpu.VMEM((2, 4, tokens, units), BF16),
            pltpu.VMEM((2, 2, 4, 2 * rows, half), BF16),
            pltpu.VMEM((2, 4, 2 * rows, half), BF16),
            pltpu.VMEM((2, 2, 2 * rows, half // 2), BF16),
            pltpu.VMEM((2, 2, 2 * rows, half), BF16),
            pltpu.VMEM((2 * rows, half), BF16),
            pltpu.VMEM((block, units), F32),
            pltpu.VMEM((rows, half), BF16),
            pltpu.VMEM((rows, half), BF16),
            pltpu.VMEM((rows, half), BF16),
            pltpu.SemaphoreType.DMA((MESSAGES,)),
            pltpu.SemaphoreType.DMA((MESSAGES,)),
            pltpu.SemaphoreType.DMA((2 * PIECES + 1,)),
        ],
        compiler_params=pltpu.CompilerParams(collective_id=0, has_side_effects=True, vmem_limit_bytes=67043328),
        name="gelu_backward",
    )(saved_inputs, hidden_grads, up_weight, up_bias.reshape(1, -1))


def solution(mesh):
    return jax.shard_map(
        body,
        mesh=mesh,
        in_specs=(P(("dp", "tensor"), None), P("dp", "tensor"), P(None, "tensor"), P("tensor")),
        out_specs=(P(("dp", "tensor"), None), P("dp", "tensor")),
        check_vma=False,
    )
```

time: 347 us -> 134 us (0.39)
  the two profiles are of different devices: /device:TPU:6 before, /device:TPU:1 now
where the time goes in v1:
time: 134 us
  Pallas kernels  127 us (95%)
  local copies, waits for them, and re-layouts  6.21 us (5%)
    pallas_call x1, Pallas kernels, body(): pl.pallas_call(functools.partial(kernel, factor), out_shape=(jax.ShapeDty...  127 us
    unnamed x2, local copies, waits for them, and re-layouts  4.92 us

profile of v1, /device:TPU:1, one launch (start us, length us, event | category | flops | bytes accessed | tf_op | source)
XLA Modules:
  0.0 133.6 jit_solution(3365181426274012793)
XLA Ops:
  0.6 1.3 reshape.7.bias_ref
  1.9 126.7 %gelu_backward.1 = (bf16[24,6144]{1,0:T(8,128)(2,1)}, bf16[768,1536]{1,0:T(8,128)(2,1)}) custom-call(bf16[24,6144]{1,0:T(8,128)(2,1)} %x_ref.1, bf16[384,1536]{1,0:T(8,128)(2,1)} %hidden_hbm.1, bf16[6144,1536]{1,0:T(8,128)(2,1)} %weight_hbm.1, f32[1,1536]{1,0:T(1,128)} %reshape.7.bias_ref), custom_call_target="tpu_custom_call" | custom-call | tf_op jit(solution)/shard_map/gelu_backward/pallas_call | solution.py:395
  128.7 1.7 %copy.8 = bf16[24,6144]{1,0:T(8,128)(2,1)} copy(bf16[24,6144]{1,0:T(8,128)(2,1)} %get-tuple-element.4) | data formatting | bytes 589824
  130.4 3.2 %copy.9 = bf16[768,1536]{1,0:T(8,128)(2,1)} copy(bf16[768,1536]{1,0:T(8,128)(2,1)} %get-tuple-element.5) | data formatting | bytes 4718592

commit v2 on v1

v2 whole, which is shorter than its diff:
```python
import functools

import jax
import jax.numpy as jnp
from jax import lax
from jax.experimental import pallas as pl
from jax.experimental.pallas import tpu as pltpu
from jax.sharding import PartitionSpec as P

MESH = pl.DeviceIdType.MESH
F32 = jnp.float32
BF16 = jnp.bfloat16

PIECES = 2
CHUNKS = 6
OWN = CHUNKS
GROUP = CHUNKS // 2

SWAP = 0
FIRST = 1
SECOND = FIRST + 17 * PIECES
EXCHANGE = SECOND + 17
GRADS = EXCHANGE + 4
HALVES = GRADS + 9 * (CHUNKS + 1)
SCATTER = HALVES + 2 * GROUP
MESSAGES = SCATTER + 10


def slope(pre):
    cdf = 0.5 * (1.0 + lax.erf(pre * 0.7071067811865476))
    pdf = jnp.exp(-0.5 * pre * pre) * 0.3989422804014327
    return cdf + pre * pdf


class Gather:
    def __init__(self, post, await_, number, view, q, p, ring, pair, twin=None, mine=0, other=0, late=lambda k: False):
        self.post, self.await_, self.number, self.view = post, await_, number, view
        self.q, self.p, self.ring, self.pair = q, p, ring, pair
        self.twin, self.mine, self.other, self.late = twin, mine, other, late

    def places(self):
        q, p = self.q, self.p
        near = [(q, p), (q + 1, p), (q, p + 3), (q, p + 1)]
        return near + [(q + 1, p + 3), (q + 1, p + 1), (q, p + 2), (q + 1, p + 2)]

    def move(self, m, k, q, p, part, device):
        view = self.view(self.mine, q % 2, p % 4, part, k)
        self.post(self.number(m, k), view, view, device)

    def landed(self, m, k, q, p, part):
        self.await_(self.number(m, k), self.view(self.mine, q % 2, p % 4, part, k))

    def hand(self, m, k, q, p):
        if self.twin is not None:
            self.move(m, k, q, p, 2, self.twin)

    def either(self, k, late, early):
        (late if self.late(k) else early)()

    def own(self, k):
        q, p = self.q, self.p
        self.move(0, k, q, p, 2, self.pair)
        self.move(1, k, q, p, 2, self.ring(1))
        self.move(2, k, q, p, 2, self.ring(3))
        self.hand(9, k, q, p)

    def paired(self, k):
        q, p = self.q + 1, self.p
        self.landed(0, k, q, p, 2)

        def early():
            self.move(3, k, q, p, 2, self.ring(1))
            self.move(4, k, q, p, 2, self.ring(3))

        self.either(k, lambda: None, early)
        self.hand(10, k, q, p)

    def halves(self, k, q, m, forward):
        p = self.p
        self.landed(m, k, q, p + 3, 2)
        self.move(forward, k, q, p + 3, 0, self.ring(1))
        self.landed(m + 1, k, q, p + 1, 2)
        self.move(forward + 1, k, q, p + 1, 1, self.ring(3))

    def near(self, k):
        q, p = self.q, self.p
        self.halves(k, q, 1, 5)

        def late():
            self.move(3, k, q, p + 3, 2, self.pair)
            self.move(4, k, q, p + 1, 2, self.pair)

        self.either(k, late, lambda: None)
        self.hand(11, k, q, p + 3)
        self.hand(12, k, q, p + 1)

    def near_paired(self, k):
        q, p = self.q + 1, self.p

        def late():
            self.landed(3, k, q, p + 3, 2)
            self.landed(4, k, q, p + 1, 2)

        self.either(k, late, lambda: self.halves(k, q, 3, 7))
        self.hand(13, k, q, p + 3)
        self.hand(14, k, q, p + 1)

    def far(self, k):
        q, p = self.q, self.p + 2
        self.landed(5, k, q, p, 0)
        self.landed(6, k, q, p, 1)
        self.either(k, lambda: self.move(7, k, q, p, 2, self.pair), lambda: None)
        self.hand(15, k, q, p)

    def far_paired(self, k):
        q, p = self.q + 1, self.p + 2

        def early():
            self.landed(7, k, q, p, 0)
            self.landed(8, k, q, p, 1)

        self.either(k, lambda: self.landed(7, k, q, p, 2), early)
        self.hand(16, k, q, p)

    def handed(self, k, first=0, last=8):
        for i, (a, b) in list(enumerate(self.places()))[first:last]:
            self.await_(self.number(9 + i, k), self.view(self.other, a % 2, b % 4, 2, k))

    def drain(self, drained, k):
        def gone(m, part):
            drained(self.number(m, k), self.view(self.mine, self.q, self.p, part, k))

        def early():
            gone(7, 0)
            gone(8, 1)

        for m, part in enumerate([2] * 5 + [0, 1]):
            gone(m, part)
        self.either(k, lambda: gone(7, 2), early)
        if self.twin is not None:
            for m in range(9, 17):
                gone(m, 2)


def kernel(
    factor, x_ref, hidden_hbm, weight_hbm, bias_ref, inputs_hbm, weights_hbm,
    weight, hidden, xr, xb, xt, grads, outgoing, partial, twin_part, near_part, next_part, pair_part, total, swap, share, final,
    inputs_out, weights_out, sends, receives, loads, stores,
):
    d, t = lax.axis_index("dp"), lax.axis_index("tensor")
    zl, x, zh, y, c = d // 4, d % 4, t // 8, (t // 2) % 4, t % 2
    o = 1 - c
    rows, model = x_ref.shape
    half = model // 2
    tokens, units = hidden.shape
    width = units // GROUP
    lines = tokens // 2
    piece = half // PIECES
    block = model // 8
    step = half // GROUP

    def at(zl_, x_, zh_, y_, c_):
        return (zl_ * 4 + x_ % 4, zh_ * 8 + (y_ % 4) * 2 + c_)

    twin = at(zl, x, zh, y, o)
    pair_h = at(zl, x, 1 - zh, y, c)
    pair_l = at(1 - zl, x, zh, y, c)

    def ring_y(k):
        return at(zl, x, zh, y + k, c)

    def ring_x(k):
        return at(zl, x + k, zh, y, c)

    def post(m, src, dst, device):
        pltpu.make_async_remote_copy(
            src_ref=src, dst_ref=dst, send_sem=sends.at[m], recv_sem=receives.at[m], device_id=device, device_id_type=MESH
        ).start()

    def described(m, ref):
        return pltpu.make_async_remote_copy(
            src_ref=ref, dst_ref=ref, send_sem=sends.at[m], recv_sem=receives.at[m], device_id=twin, device_id_type=MESH
        )

    def landed(m, ref):
        described(m, ref).wait_recv()

    def drained(m, ref):
        described(m, ref).wait_send()

    def weight_load(j, h):
        part = pl.ds(h * half + j * piece, piece)
        return pltpu.make_async_copy(weight_hbm.at[part], weight.at[part], loads.at[2 * j + h])

    for j in range(PIECES):
        for h in range(2):
            weight_load(j, h).start()
    places = [(zh, y), (zh + 1, y), (zh, y + 3), (zh, y + 1), (zh + 1, y + 3), (zh + 1, y + 1), (zh, y + 2), (zh + 1, y + 2)]
    places = [(a % 2, b % 4) for a, b in places]
    hidden_loads = []
    for i, (a, b) in enumerate(places):
        source = pl.ds(pl.multiple_of((a * 4 + b) * (2 * rows), 2 * rows), 2 * rows)
        load = pltpu.make_async_copy(
            hidden_hbm.at[source], hidden.at[pl.ds(i * 2 * rows, 2 * rows)], loads.at[2 * PIECES + i]
        )
        load.start()
        hidden_loads.append(load)

    barrier = pltpu.get_barrier_semaphore()
    greeted = [twin, pair_h, pair_l, ring_y(1), ring_y(3), ring_x(1), ring_x(3)]
    greeted += [at(o, x + k, zh, y, zl) for k in range(4)]
    for device in greeted:
        pl.semaphore_signal(barrier, inc=1, device_id=device, device_id_type=MESH)
    pl.semaphore_wait(barrier, len(greeted))

    own_half = pl.ds(pl.multiple_of(c * half, half), half)
    other_half = pl.ds(pl.multiple_of(o * half, half), half)
    post(SWAP, x_ref.at[:, other_half], swap, twin)
    mine = x_ref[:, own_half].astype(F32)
    landed(SWAP, swap)
    theirs = swap[...].astype(F32)
    upper = jnp.where(c == 0, mine, theirs)
    lower = jnp.where(c == 0, theirs, mine)
    xr[c, zh, y] = jnp.concatenate([upper, lower], axis=0).astype(BF16)

    def late(k):
        return k % GROUP == 1 and k != OWN

    def view_first(h, q, p, part, j):
        cols = (pl.ds(j * piece, piece // 2), pl.ds(j * piece + piece // 2, piece // 2), pl.ds(j * piece, piece))[part]
        return xr.at[h, q, p, :, cols]

    def view_second(h, q, p, part, j):
        return xb.at[h, q, p, (pl.ds(0, 2), pl.ds(2, 2), pl.ds(0, 4))[part]]

    def view_grads(h, q, p, part, k):
        if k == OWN:
            start, stop, column, wide = 0, 2 * rows, 0, units
        else:
            start, stop = ((2 * rows, lines), (lines, tokens))[k // GROUP]
            column, wide = k % GROUP * width, width
        begin, size = ((0, wide // 2), (wide // 2, wide // 2), (0, wide))[part]
        return grads.at[q, p, pl.ds(start, stop - start), pl.ds(column + begin, size)]

    first = Gather(post, landed, lambda m, j: FIRST + 17 * j + m, view_first, zh, y, ring_y, pair_h, twin, c, o)
    second = Gather(post, landed, lambda m, j: SECOND + m, view_second, zh, y, ring_y, pair_h, twin, o, c)
    third = Gather(post, landed, lambda m, k: GRADS + (CHUNKS + 1) * m + k, view_grads, zl, x, ring_x, pair_l, late=late)

    for j in range(PIECES):
        first.own(j)

    for j in range(PIECES):
        first.handed(j, 0, 1)
    for j in range(PIECES):
        for h in range(2):
            weight_load(j, h).wait()
    for load in hidden_loads:
        load.wait()

    narrow = width // 2
    strip = 2 * rows

    def forward(start, stop, n):
        @pl.loop(2 * n, 2 * n + 2)
        def _(i):
            cols = pl.ds(pl.multiple_of(i * narrow, narrow), narrow)
            pre = bias_ref[cols].reshape(1, narrow)
            for h in range(2):
                a = jnp.concatenate([xr[h, a, b] for a, b in places[start:stop]], axis=0)
                pre = pre + jnp.dot(a, weight[h * half : (h + 1) * half, cols], preferred_element_type=F32)
            total[0 : (stop - start) * strip, 0:narrow] = pre

            @pl.loop(0, stop - start)
            def _(s):
                here = pl.ds(pl.multiple_of(s * strip, strip), strip)
                there = pl.ds(pl.multiple_of((start + s) * strip, strip), strip)
                g = hidden[there, cols].astype(F32) * slope(total[here, 0:narrow])
                grads[zl, x, there, cols] = g.astype(BF16)

    for n in range(GROUP):
        forward(0, 1, n)
    third.own(OWN)
    for j in range(PIECES):
        first.paired(j)
        first.near(j)
    for k in range(4):
        cols = pl.ds(pl.multiple_of(((x + k) % 4) * block, block), block)
        post(EXCHANGE + k, xr.at[c, zh, y, :, cols], xb.at[zl, zh, y, x], at(c, x + k, zh, y, 1 - zl))
    for j in range(PIECES):
        first.handed(j, 1, 4)

    thin = step // 4
    slots = (0, 1, 2, 4, 3, 5, 6, 7)

    def backward(h, group, n):
        part = pl.ds(pl.multiple_of(h * half + n * thin, thin), thin)
        g = grads[zl, x, group * lines : (group + 1) * lines, :]
        return lax.dot_general(g, weight[part, :], (((1,), (1,)), ((), ())), preferred_element_type=F32)

    def rows_of(group):
        return pl.ds(group * lines, lines)

    def piece_of(n):
        return pl.ds(pl.multiple_of(n * thin, thin), thin)

    def chunk_of(k):
        return pl.ds(pl.multiple_of(k * step, step), step)

    def backward_other(group, k):
        @pl.loop(4 * k, 4 * k + 4)
        def _(n):
            outgoing[rows_of(group), piece_of(n)] = backward(o, group, n).astype(BF16)

        here = (rows_of(group), chunk_of(k))
        post(HALVES + group * GROUP + k, outgoing.at[here], twin_part.at[here], twin)

    def backward_own(group, k):
        landed(HALVES + group * GROUP + k, twin_part.at[rows_of(group), chunk_of(k)])

        @pl.loop(4 * k, 4 * k + 4)
        def _(n):
            value = backward(c, group, n) + twin_part[rows_of(group), piece_of(n)].astype(F32)
            for i in range(4):
                partial[slots[4 * group + i], :, piece_of(n)] = value[i * 2 * rows : (i + 1) * 2 * rows].astype(BF16)

    near_replicas = [(zl, x), (zl + 1, x), (zl, x + 3), (zl, x + 1)]
    far_replicas = [(zl, x + 2), (zl + 1, x + 3), (zl + 1, x + 1), (zl + 1, x + 2)]

    def turn(replicas, group):
        for i, (q, p) in enumerate(replicas):
            some = places[4 * group : 4 * group + 4]
            block_rows = jnp.concatenate([xb[q % 2, a, b, p % 4] for a, b in some], axis=0)
            xt[:, i * lines : (i + 1) * lines] = block_rows.T

    def outer(replicas, group, n):
        cols = pl.ds(pl.multiple_of(n * narrow, narrow), narrow)
        g = jnp.concatenate([grads[q % 2, p % 4, group * lines : (group + 1) * lines, cols] for q, p in replicas], axis=0)
        return cols, jnp.dot(xt[...], g, preferred_element_type=F32)

    def add(replicas, group, start=False):
        turn(replicas, group)

        @pl.loop(0, 2 * GROUP)
        def _(n):
            cols, term = outer(replicas, group, n)
            if start:
                total[:, cols] = term
            else:
                total[:, cols] += term

    left, right = pl.ds(0, half // 2), pl.ds(half // 2, half // 2)
    minus, plus, across = pl.ds(2, 2), pl.ds(4, 2), pl.ds(6, 2)

    third.paired(OWN)
    third.near(OWN)
    forward(1, 4, 0)
    third.own(0)
    forward(1, 4, 1)
    third.own(1)
    first.near_paired(0)
    forward(1, 4, 2)
    third.own(2)
    for k in range(4):
        landed(EXCHANGE + k, xb.at[o, zh, y, (x + 4 - k) % 4])
    second.own(0)
    backward_other(0, 0)
    first.near_paired(1)
    backward_other(0, 1)
    third.paired(0)
    third.near(0)
    backward_other(0, 2)
    for j in range(PIECES):
        first.far(j)
    backward_own(0, 0)
    backward_own(0, 1)
    backward_own(0, 2)
    for j in range(PIECES):
        first.far_paired(j)
    third.near(1)
    third.paired(1)
    post(SCATTER + 2, partial.at[4, :, right], next_part.at[0, 0, :, right], ring_y(1))
    post(SCATTER + 3, partial.at[2, :, left], next_part.at[1, 0, :, left], ring_y(3))
    for j in range(PIECES):
        first.handed(j, 4, 8)
    forward(4, 8, 0)
    third.own(3)
    third.paired(2)
    third.near(2)
    forward(4, 8, 1)
    third.own(4)
    second.paired(0)
    second.near(0)
    forward(4, 8, 2)
    third.own(5)
    third.near_paired(0)
    third.near_paired(OWN)
    third.far(OWN)
    third.far(0)
    backward_other(1, 0)
    third.far(1)
    backward_other(1, 1)
    backward_other(1, 2)
    backward_own(1, 0)
    third.paired(3)
    third.near(3)
    backward_own(1, 1)
    backward_own(1, 2)

    post(SCATTER + 0, partial.at[across, :, left], near_part.at[0], ring_y(1))
    post(SCATTER + 1, partial.at[across, :, right], near_part.at[1], ring_y(3))
    second.near_paired(0)
    second.far(0)
    second.far_paired(0)
    third.near_paired(2)
    third.far(2)
    second.handed(0)
    add(near_replicas, 0, True)
    third.near(4)
    third.paired(4)
    landed(SCATTER + 0, near_part.at[0])
    partial[plus, :, left] = (partial[plus, :, left].astype(F32) + near_part[0].astype(F32)).astype(BF16)
    post(SCATTER + 4, partial.at[plus, :, left], next_part.at[0, :, :, left], ring_y(1))
    landed(SCATTER + 1, near_part.at[1])
    partial[minus, :, right] = (partial[minus, :, right].astype(F32) + near_part[1].astype(F32)).astype(BF16)
    post(SCATTER + 5, partial.at[minus, :, right], next_part.at[1, :, :, right], ring_y(3))
    post(SCATTER + 8, partial.at[5, :, right], next_part.at[0, 1, :, right], ring_y(1))
    post(SCATTER + 9, partial.at[3, :, left], next_part.at[1, 1, :, left], ring_y(3))
    third.paired(5)
    third.near(5)
    add(near_replicas, 1)
    third.near_paired(3)
    third.far(3)

    third.far(4)
    third.near_paired(1)
    landed(SCATTER + 2, next_part.at[0, 0, :, right])
    landed(SCATTER + 3, next_part.at[1, 0, :, left])
    landed(SCATTER + 8, next_part.at[0, 1, :, right])
    landed(SCATTER + 9, next_part.at[1, 1, :, left])
    landed(SCATTER + 4, next_part.at[0, :, :, left])
    landed(SCATTER + 5, next_part.at[1, :, :, right])

    def reduced(z):
        return partial[z].astype(F32) + next_part[0, z].astype(F32) + next_part[1, z].astype(F32)

    partial[1] = reduced(1).astype(BF16)
    post(SCATTER + 6, partial.at[1], pair_part, pair_h)

    third.near_paired(5)
    third.far_paired(OWN)
    third.far_paired(0)
    third.far_paired(1)
    third.far_paired(2)
    add(far_replicas, 0)
    third.far(5)
    landed(SCATTER + 6, pair_part)
    summed = reduced(0) + pair_part[...].astype(F32)
    upper, lower = summed[0:rows], summed[rows : 2 * rows]
    share[...] = jnp.where(c == 0, lower, upper).astype(BF16)
    post(SCATTER + 7, share, final, twin)
    inputs_out[:, own_half] = jnp.where(c == 0, upper, lower).astype(BF16)

    def weight_store(i):
        cols = pl.ds(pl.multiple_of(i * narrow, narrow), narrow)
        return pltpu.make_async_copy(weights_out.at[:, cols], weights_hbm.at[:, cols], stores.at[i])

    third.near_paired(4)
    turn(far_replicas, 1)

    for k in range(GROUP):
        third.far_paired(GROUP + k)

        @pl.loop(2 * k, 2 * k + 2)
        def _(n):
            cols, term = outer(far_replicas, 1, n)
            weights_out[:, cols] = ((total[:, cols] + term) * factor).astype(BF16)
            weight_store(n).start()

    landed(SCATTER + 7, final)
    inputs_out[:, other_half] = final[...]
    inputs_store = pltpu.make_async_copy(inputs_out, inputs_hbm, stores.at[2 * GROUP])
    inputs_store.start()


    @pl.loop(0, 2 * GROUP)
    def _(i):
        weight_store(i).wait()

    inputs_store.wait()
    drained(SWAP, swap)
    for j in range(PIECES):
        first.drain(drained, j)
    second.drain(drained, 0)
    for k in range(4):
        drained(EXCHANGE + k, xb.at[zl, zh, y, x])

    for k in range(CHUNKS + 1):
        third.drain(drained, k)
    for k in range(2 * GROUP):
        drained(HALVES + k, twin_part.at[rows_of(0), chunk_of(0)])

    for m, ref in enumerate(
        [
            near_part.at[0], near_part.at[1], next_part.at[0, 0, :, right], next_part.at[1, 0, :, left],
            next_part.at[0, :, :, left], next_part.at[1, :, :, right], pair_part, share,
            next_part.at[0, 1, :, right], next_part.at[1, 1, :, left],
        ]
    ):
        drained(SCATTER + m, ref)


def body(saved_inputs, hidden_grads, up_weight, up_bias):
    rows, model = saved_inputs.shape
    tokens, units = hidden_grads.shape
    half, block = model // 2, model // 8
    factor = float(1.0 / (tokens * 8) ** 0.5)
    any_space, vmem = pl.BlockSpec(memory_space=pl.ANY), pl.BlockSpec(memory_space=pltpu.VMEM)
    return pl.pallas_call(
        functools.partial(kernel, factor),
        out_shape=(jax.ShapeDtypeStruct((rows, model), BF16), jax.ShapeDtypeStruct((block, units), BF16)),
        in_specs=[vmem, any_space, any_space, vmem],
        out_specs=(any_space, any_space),
        scratch_shapes=[
            pltpu.VMEM((model, units), BF16),
            pltpu.VMEM((tokens, units), BF16),
            pltpu.VMEM((2, 2, 4, 2 * rows, half), BF16),
            pltpu.VMEM((2, 2, 4, 4, 2 * rows, block), BF16),
            pltpu.VMEM((block, 2 * tokens), BF16),
            pltpu.VMEM((2, 4, tokens, units), BF16),
            pltpu.VMEM((tokens, half), BF16),
            pltpu.VMEM((8, 2 * rows, half), BF16),
            pltpu.VMEM((tokens, half), BF16),
            pltpu.VMEM((2, 2, 2 * rows, half // 2), BF16),
            pltpu.VMEM((2, 2, 2 * rows, half), BF16),
            pltpu.VMEM((2 * rows, half), BF16),
            pltpu.VMEM((block, units), F32),
            pltpu.VMEM((rows, half), BF16),
            pltpu.VMEM((rows, half), BF16),
            pltpu.VMEM((rows, half), BF16),
            pltpu.VMEM((rows, model), BF16),
            pltpu.VMEM((block, units), BF16),
            pltpu.SemaphoreType.DMA((MESSAGES,)),
            pltpu.SemaphoreType.DMA((MESSAGES,)),
            pltpu.SemaphoreType.DMA((2 * PIECES + 8,)),
            pltpu.SemaphoreType.DMA((2 * GROUP + 1,)),
        ],
        compiler_params=pltpu.CompilerParams(collective_id=0, has_side_effects=True, vmem_limit_bytes=62000000),
        name="gelu_backward",
    )(saved_inputs, hidden_grads, up_weight, up_bias)


def solution(mesh):
    return jax.shard_map(
        body,
        mesh=mesh,
        in_specs=(P(("dp", "tensor"), None), P("dp", "tensor"), P(None, "tensor"), P("tensor")),
        out_specs=(P(("dp", "tensor"), None), P("dp", "tensor")),
        check_vma=False,
    )
```

time: 134 us -> 110 us (0.82)
  Pallas kernels: 127 us -> 104 us
    pallas_call x1, Pallas kernels: 127 us -> 104 us  [body(): pl.pallas_call(functools.partial(kernel, factor), out_shape=(jax.ShapeDty...]
where the time goes in v2:
time: 110 us
  Pallas kernels  104 us (95%)
  local copies, waits for them, and re-layouts  4.92 us (4%)
    pallas_call x1, Pallas kernels, body(): pl.pallas_call(functools.partial(kernel, factor), out_shape=(jax.ShapeDty...  104 us
    unnamed x2, local copies, waits for them, and re-layouts  4.92 us

profile of v2, /device:TPU:1, one launch (start us, length us, event | category | flops | bytes accessed | tf_op | source)
XLA Modules:
  0.0 109.7 jit_solution(14762942811838677600)
XLA Ops:
  0.6 104.2 %gelu_backward.1 = (bf16[24,6144]{1,0:T(8,128)(2,1)}, bf16[768,1536]{1,0:T(8,128)(2,1)}) custom-call(bf16[24,6144]{1,0:T(8,128)(2,1)} %x_ref.1, bf16[384,1536]{1,0:T(8,128)(2,1)} %hidden_hbm.1, bf16[6144,1536]{1,0:T(8,128)(2,1)} %weight_hbm.1, f32[1536]{0:T(1024)} %bias_ref.1), custom_call_target="tpu_custom_call" | custom-call | tf_op jit(solution)/shard_map/gelu_backward/pallas_call | solution.py:518
  104.8 1.7 %copy.8 = bf16[24,6144]{1,0:T(8,128)(2,1)} copy(bf16[24,6144]{1,0:T(8,128)(2,1)} %get-tuple-element.4) | data formatting | bytes 589824
  106.5 3.2 %copy.9 = bf16[768,1536]{1,0:T(8,128)(2,1)} copy(bf16[768,1536]{1,0:T(8,128)(2,1)} %get-tuple-element.5) | data formatting | bytes 4718592

commit v3 on v2

--- a/solution.py
+++ b/solution.py
@@ -143,9 +143,9 @@
 
 
 def kernel(
-    factor, x_ref, hidden_hbm, weight_hbm, bias_ref, inputs_hbm, weights_hbm,
+    factor, x_ref, hidden_hbm, weight_hbm, bias_ref, inputs_out, weights_out,
     weight, hidden, xr, xb, xt, grads, outgoing, partial, twin_part, near_part, next_part, pair_part, total, swap, share, final,
-    inputs_out, weights_out, sends, receives, loads, stores,
+    sends, receives, loads,
 ):
     d, t = lax.axis_index("dp"), lax.axis_index("tensor")
     zl, x, zh, y, c = d // 4, d % 4, t // 8, (t // 2) % 4, t % 2
@@ -224,7 +224,7 @@
     xr[c, zh, y] = jnp.concatenate([upper, lower], axis=0).astype(BF16)
 
     def late(k):
-        return k % GROUP == 1 and k != OWN
+        return k in (1, GROUP)
 
     def view_first(h, q, p, part, j):
         cols = (pl.ds(j * piece, piece // 2), pl.ds(j * piece + piece // 2, piece // 2), pl.ds(j * piece, piece))[part]
@@ -280,12 +280,12 @@
     for n in range(GROUP):
         forward(0, 1, n)
     third.own(OWN)
-    for j in range(PIECES):
-        first.paired(j)
-        first.near(j)
     for k in range(4):
         cols = pl.ds(pl.multiple_of(((x + k) % 4) * block, block), block)
         post(EXCHANGE + k, xr.at[c, zh, y, :, cols], xb.at[zl, zh, y, x], at(c, x + k, zh, y, 1 - zl))
+    for j in range(PIECES):
+        first.paired(j)
+        first.near(j)
     for j in range(PIECES):
         first.handed(j, 1, 4)
 
@@ -356,28 +356,30 @@
     forward(1, 4, 0)
     third.own(0)
     forward(1, 4, 1)
+    for k in range(4):
+        landed(EXCHANGE + k, xb.at[o, zh, y, (x + 4 - k) % 4])
+    second.own(0)
     third.own(1)
     first.near_paired(0)
     forward(1, 4, 2)
     third.own(2)
-    for k in range(4):
-        landed(EXCHANGE + k, xb.at[o, zh, y, (x + 4 - k) % 4])
-    second.own(0)
     backward_other(0, 0)
     first.near_paired(1)
     backward_other(0, 1)
+    backward_other(0, 2)
     third.paired(0)
     third.near(0)
-    backward_other(0, 2)
     for j in range(PIECES):
         first.far(j)
     backward_own(0, 0)
     backward_own(0, 1)
     backward_own(0, 2)
-    for j in range(PIECES):
-        first.far_paired(j)
     third.near(1)
     third.paired(1)
+    second.paired(0)
+    second.near(0)
+    for j in range(PIECES):
+        first.far_paired(j)
     post(SCATTER + 2, partial.at[4, :, right], next_part.at[0, 0, :, right], ring_y(1))
     post(SCATTER + 3, partial.at[2, :, left], next_part.at[1, 0, :, left], ring_y(3))
     for j in range(PIECES):
@@ -388,8 +390,6 @@
     third.near(2)
     forward(4, 8, 1)
     third.own(4)
-    second.paired(0)
-    second.near(0)
     forward(4, 8, 2)
     third.own(5)
     third.near_paired(0)
@@ -398,19 +398,21 @@
     third.far(0)
     backward_other(1, 0)
     third.far(1)
+    second.near_paired(0)
+    second.far(0)
     backward_other(1, 1)
+    third.paired(3)
+    third.near(3)
     backward_other(1, 2)
     backward_own(1, 0)
-    third.paired(3)
-    third.near(3)
+    second.far_paired(0)
     backward_own(1, 1)
     backward_own(1, 2)
 
     post(SCATTER + 0, partial.at[across, :, left], near_part.at[0], ring_y(1))
     post(SCATTER + 1, partial.at[across, :, right], near_part.at[1], ring_y(3))
-    second.near_paired(0)
-    second.far(0)
-    second.far_paired(0)
+    post(SCATTER + 8, partial.at[5, :, right], next_part.at[0, 1, :, right], ring_y(1))
+    post(SCATTER + 9, partial.at[3, :, left], next_part.at[1, 1, :, left], ring_y(3))
     third.near_paired(2)
     third.far(2)
     second.handed(0)
@@ -423,15 +425,12 @@
     landed(SCATTER + 1, near_part.at[1])
     partial[minus, :, right] = (partial[minus, :, right].astype(F32) + near_part[1].astype(F32)).astype(BF16)
     post(SCATTER + 5, partial.at[minus, :, right], next_part.at[1, :, :, right], ring_y(3))
-    post(SCATTER + 8, partial.at[5, :, right], next_part.at[0, 1, :, right], ring_y(1))
-    post(SCATTER + 9, partial.at[3, :, left], next_part.at[1, 1, :, left], ring_y(3))
+    third.far(3)
     third.paired(5)
     third.near(5)
     add(near_replicas, 1)
-    third.near_paired(3)
-    third.far(3)
-
-    third.far(4)
+
+    third.near_paired(4)
     third.near_paired(1)
     landed(SCATTER + 2, next_part.at[0, 0, :, right])
     landed(SCATTER + 3, next_part.at[1, 0, :, left])
@@ -452,6 +451,7 @@
     third.far_paired(1)
     third.far_paired(2)
     add(far_replicas, 0)
+    third.far(4)
     third.far(5)
     landed(SCATTER + 6, pair_part)
     summed = reduced(0) + pair_part[...].astype(F32)
@@ -460,11 +460,7 @@
     post(SCATTER + 7, share, final, twin)
     inputs_out[:, own_half] = jnp.where(c == 0, upper, lower).astype(BF16)
 
-    def weight_store(i):
-        cols = pl.ds(pl.multiple_of(i * narrow, narrow), narrow)
-        return pltpu.make_async_copy(weights_out.at[:, cols], weights_hbm.at[:, cols], stores.at[i])
-
-    third.near_paired(4)
+    third.near_paired(3)
     turn(far_replicas, 1)
 
     for k in range(GROUP):
@@ -474,19 +470,9 @@
         def _(n):
             cols, term = outer(far_replicas, 1, n)
             weights_out[:, cols] = ((total[:, cols] + term) * factor).astype(BF16)
-            weight_store(n).start()
 
     landed(SCATTER + 7, final)
     inputs_out[:, other_half] = final[...]
-    inputs_store = pltpu.make_async_copy(inputs_out, inputs_hbm, stores.at[2 * GROUP])
-    inputs_store.start()
-
-
-    @pl.loop(0, 2 * GROUP)
-    def _(i):
-        weight_store(i).wait()
-
-    inputs_store.wait()
     drained(SWAP, swap)
     for j in range(PIECES):
         first.drain(drained, j)
@@ -517,9 +503,9 @@
     any_space, vmem = pl.BlockSpec(memory_space=pl.ANY), pl.BlockSpec(memory_space=pltpu.VMEM)
     return pl.pallas_call(
         functools.partial(kernel, factor),
-        out_shape=(jax.ShapeDtypeStruct((rows, model), BF16), jax.ShapeDtypeStruct((block, units), BF16)),
+        out_shape=(pltpu.VMEM((rows, model), BF16), pltpu.VMEM((block, units), BF16)),
         in_specs=[vmem, any_space, any_space, vmem],
-        out_specs=(any_space, any_space),
+        out_specs=(vmem, vmem),
         scratch_shapes=[
             pltpu.VMEM((model, units), BF16),
             pltpu.VMEM((tokens, units), BF16),
@@ -537,12 +523,9 @@
             pltpu.VMEM((rows, half), BF16),
             pltpu.VMEM((rows, half), BF16),
             pltpu.VMEM((rows, half), BF16),
-            pltpu.VMEM((rows, model), BF16),
-            pltpu.VMEM((block, units), BF16),
             pltpu.SemaphoreType.DMA((MESSAGES,)),
             pltpu.SemaphoreType.DMA((MESSAGES,)),
             pltpu.SemaphoreType.DMA((2 * PIECES + 8,)),
-            pltpu.SemaphoreType.DMA((2 * GROUP + 1,)),
         ],
         compiler_params=pltpu.CompilerParams(collective_id=0, has_side_effects=True, vmem_limit_bytes=62000000),
         name="gelu_backward",

time: 110 us -> 95.3 us (0.87)
  Pallas kernels: 104 us -> 92.2 us
  local copies, waits for them, and re-layouts: 4.92 us -> 2.12 us
    pallas_call x1, Pallas kernels: 104 us -> 92.2 us  [body(): pl.pallas_call(functools.partial(kernel, factor), out_shape=(pltpu.VMEM((...]
    unnamed x2, local copies, waits for them, and re-layouts: 4.92 us -> 2.12 us
where the time goes in v3:
time: 95.3 us; the launch traced here: 94.9 us
  Pallas kernels  92.2 us (97%)
  local copies, waits for them, and re-layouts  2.12 us (2%)
    pallas_call x1, Pallas kernels, body(): pl.pallas_call(functools.partial(kernel, factor), out_shape=(pltpu.VMEM((...  92.2 us
    unnamed x2, local copies, waits for them, and re-layouts  2.12 us

profile of v3, /device:TPU:1, one launch (start us, length us, event | category | flops | bytes accessed | tf_op | source)
XLA Modules:
  0.0 94.9 jit_solution(1899960810182244398)
XLA Ops:
  0.6 92.2 %gelu_backward.1 = (bf16[24,6144]{1,0:T(8,128)(2,1)S(1)}, bf16[768,1536]{1,0:T(8,128)(2,1)S(1)}) custom-call(bf16[24,6144]{1,0:T(8,128)(2,1)} %x_ref.1, bf16[384,1536]{1,0:T(8,128)(2,1)} %hidden_hbm.1, bf16[6144,1536]{1,0:T(8,128)(2,1)} %weight_hbm.1, f32[1536]{0:T(1024)} %bias_ref.1), custom_call_target="tpu_custom_call" | custom-call | tf_op jit(solution)/shard_map/gelu_backward/pallas_call | solution.py:504
  92.8 0.7 copy.8
  93.5 1.4 %copy.9 = bf16[768,1536]{1,0:T(8,128)(2,1)} copy(bf16[768,1536]{1,0:T(8,128)(2,1)S(1)} %get-tuple-element.3) | data formatting | bytes 4718592

commit v4 on v3

--- a/solution.py
+++ b/solution.py
@@ -23,7 +23,7 @@
 GRADS = EXCHANGE + 4
 HALVES = GRADS + 9 * (CHUNKS + 1)
 SCATTER = HALVES + 2 * GROUP
-MESSAGES = SCATTER + 10
+MESSAGES = SCATTER + 14
 
 
 def slope(pre):
@@ -349,7 +349,6 @@
                 total[:, cols] += term
 
     left, right = pl.ds(0, half // 2), pl.ds(half // 2, half // 2)
-    minus, plus, across = pl.ds(2, 2), pl.ds(4, 2), pl.ds(6, 2)
 
     third.paired(OWN)
     third.near(OWN)
@@ -409,50 +408,58 @@
     backward_own(1, 1)
     backward_own(1, 2)
 
-    post(SCATTER + 0, partial.at[across, :, left], near_part.at[0], ring_y(1))
-    post(SCATTER + 1, partial.at[across, :, right], near_part.at[1], ring_y(3))
+    post(SCATTER + 0, partial.at[7, :, left], near_part.at[0, 1], ring_y(1))
+    post(SCATTER + 1, partial.at[7, :, right], near_part.at[1, 1], ring_y(3))
     post(SCATTER + 8, partial.at[5, :, right], next_part.at[0, 1, :, right], ring_y(1))
     post(SCATTER + 9, partial.at[3, :, left], next_part.at[1, 1, :, left], ring_y(3))
+    post(SCATTER + 10, partial.at[6, :, left], near_part.at[0, 0], ring_y(1))
+    post(SCATTER + 11, partial.at[6, :, right], near_part.at[1, 0], ring_y(3))
     third.near_paired(2)
     third.far(2)
     second.handed(0)
     add(near_replicas, 0, True)
     third.near(4)
     third.paired(4)
-    landed(SCATTER + 0, near_part.at[0])
-    partial[plus, :, left] = (partial[plus, :, left].astype(F32) + near_part[0].astype(F32)).astype(BF16)
-    post(SCATTER + 4, partial.at[plus, :, left], next_part.at[0, :, :, left], ring_y(1))
-    landed(SCATTER + 1, near_part.at[1])
-    partial[minus, :, right] = (partial[minus, :, right].astype(F32) + near_part[1].astype(F32)).astype(BF16)
-    post(SCATTER + 5, partial.at[minus, :, right], next_part.at[1, :, :, right], ring_y(3))
-    third.far(3)
     third.paired(5)
     third.near(5)
+    def pass_on(m, slot, side, i, z, device):
+        landed(m, near_part.at[i, z])
+        partial[slot, :, side] = (partial[slot, :, side].astype(F32) + near_part[i, z].astype(F32)).astype(BF16)
+        post(m + 4 if z else m + 2, partial.at[slot, :, side], next_part.at[i, z, :, side], device)
+
+    pass_on(SCATTER + 0, 5, left, 0, 1, ring_y(1))
+    pass_on(SCATTER + 1, 3, right, 1, 1, ring_y(3))
     add(near_replicas, 1)
+    third.far(3)
+    pass_on(SCATTER + 10, 4, left, 0, 0, ring_y(1))
+    pass_on(SCATTER + 11, 2, right, 1, 0, ring_y(3))
+
+    landed(SCATTER + 8, next_part.at[0, 1, :, right])
+    landed(SCATTER + 9, next_part.at[1, 1, :, left])
+    landed(SCATTER + 4, next_part.at[0, 1, :, left])
+    landed(SCATTER + 5, next_part.at[1, 1, :, right])
+
+    def reduced(z):
+        return partial[z].astype(F32) + next_part[0, z].astype(F32) + next_part[1, z].astype(F32)
+
+    partial[1] = reduced(1).astype(BF16)
+    post(SCATTER + 6, partial.at[1], pair_part, pair_h)
 
     third.near_paired(4)
     third.near_paired(1)
-    landed(SCATTER + 2, next_part.at[0, 0, :, right])
-    landed(SCATTER + 3, next_part.at[1, 0, :, left])
-    landed(SCATTER + 8, next_part.at[0, 1, :, right])
-    landed(SCATTER + 9, next_part.at[1, 1, :, left])
-    landed(SCATTER + 4, next_part.at[0, :, :, left])
-    landed(SCATTER + 5, next_part.at[1, :, :, right])
-
-    def reduced(z):
-        return partial[z].astype(F32) + next_part[0, z].astype(F32) + next_part[1, z].astype(F32)
-
-    partial[1] = reduced(1).astype(BF16)
-    post(SCATTER + 6, partial.at[1], pair_part, pair_h)
-
-    third.near_paired(5)
     third.far_paired(OWN)
     third.far_paired(0)
     third.far_paired(1)
     third.far_paired(2)
     add(far_replicas, 0)
+    turn(far_replicas, 1)
+    third.near_paired(5)
     third.far(4)
     third.far(5)
+    landed(SCATTER + 2, next_part.at[0, 0, :, right])
+    landed(SCATTER + 3, next_part.at[1, 0, :, left])
+    landed(SCATTER + 12, next_part.at[0, 0, :, left])
+    landed(SCATTER + 13, next_part.at[1, 0, :, right])
     landed(SCATTER + 6, pair_part)
     summed = reduced(0) + pair_part[...].astype(F32)
     upper, lower = summed[0:rows], summed[rows : 2 * rows]
@@ -461,7 +468,6 @@
     inputs_out[:, own_half] = jnp.where(c == 0, upper, lower).astype(BF16)
 
     third.near_paired(3)
-    turn(far_replicas, 1)
 
     for k in range(GROUP):
         third.far_paired(GROUP + k)
@@ -487,9 +493,10 @@
 
     for m, ref in enumerate(
         [
-            near_part.at[0], near_part.at[1], next_part.at[0, 0, :, right], next_part.at[1, 0, :, left],
-            next_part.at[0, :, :, left], next_part.at[1, :, :, right], pair_part, share,
-            next_part.at[0, 1, :, right], next_part.at[1, 1, :, left],
+            near_part.at[0, 1], near_part.at[1, 1], next_part.at[0, 0, :, right], next_part.at[1, 0, :, left],
+            next_part.at[0, 1, :, left], next_part.at[1, 1, :, right], pair_part, share,
+            next_part.at[0, 1, :, right], next_part.at[1, 1, :, left], near_part.at[0, 0], near_part.at[1, 0],
+            next_part.at[0, 0, :, left], next_part.at[1, 0, :, right],
         ]
     ):
         drained(SCATTER + m, ref)

time: 95.3 us -> 92.3 us (0.969)
  Pallas kernels: 92.2 us -> 89.4 us
    pallas_call x1, Pallas kernels: 92.2 us -> 89.4 us  [body(): pl.pallas_call(functools.partial(kernel, factor), out_shape=(pltpu.VMEM((...]
where the time goes in v4:
time: 92.3 us; the launch traced here: 92.2 us
  Pallas kernels  89.4 us (97%)
  local copies, waits for them, and re-layouts  2.12 us (2%)
    pallas_call x1, Pallas kernels, body(): pl.pallas_call(functools.partial(kernel, factor), out_shape=(pltpu.VMEM((...  89.4 us
    unnamed x2, local copies, waits for them, and re-layouts  2.12 us

profile of v4, /device:TPU:1, one launch (start us, length us, event | category | flops | bytes accessed | tf_op | source)
XLA Modules:
  0.0 92.2 jit_solution(13056096290172197032)
XLA Ops:
  0.6 89.4 %gelu_backward.1 = (bf16[24,6144]{1,0:T(8,128)(2,1)S(1)}, bf16[768,1536]{1,0:T(8,128)(2,1)S(1)}) custom-call(bf16[24,6144]{1,0:T(8,128)(2,1)} %x_ref.1, bf16[384,1536]{1,0:T(8,128)(2,1)} %hidden_hbm.1, bf16[6144,1536]{1,0:T(8,128)(2,1)} %weight_hbm.1, f32[1536]{0:T(1024)} %bias_ref.1), custom_call_target="tpu_custom_call" | custom-call | tf_op jit(solution)/shard_map/gelu_backward/pallas_call | solution.py:511
  90.1 0.7 copy.8
  90.8 1.4 %copy.9 = bf16[768,1536]{1,0:T(8,128)(2,1)} copy(bf16[768,1536]{1,0:T(8,128)(2,1)S(1)} %get-tuple-element.3) | data formatting | bytes 4718592
